TPU v7x, 32 devices: a whole 2x2x4 slice. The times are simulated.
32 devices in a mesh: view: 4 (over z), cell: 8 (over y, x, core).
Axes of the slice: x: 2, y: 2, z: 4, core: 2. Of those that a mesh axis runs over, the one named last changes fastest.
Arguments:
- params: float32 [59, 65536], P(None, 'cell'), may hold values from -6.22 to 3.2, as said below
- camera: float32 [4, 11], P('view'), may hold values from -0.3 to 1536, as said below
- targets: float32 [4, 256, 3, 256], P('view', 'cell'), may hold values from 0 to 1
- send_blocks: int32 [4, 8, 8, 16], P('view', 'cell'), may hold values from 0 to 255, as said below
- tile_blocks: int32 [4, 256, 16], P('view', 'cell'), may hold values from -1 to 127, as said below
- tile_order: int32 [4, 256, 512], P('view', 'cell'), may hold values from 0 to 511, as said below
Outputs:
- image: float32 [4, 256, 3, 256], P('view', 'cell')
- grads: float32 [59, 65536], P(None, 'cell')
Inputs may be any that keep to these rules, and one draw needn't show every extreme that they name: `params`: rows 0 to 2 lie in -3.2 to 3.2, rows 3 to 5 in log 0.002 to log 0.025, row 6 in 1 to 2, rows 7 to 9 in -1 to 1, row 10 in -3 to 2, rows 11 to 58 in -1.5 to 1.5. `camera`: quaternion first entry 1 to 2, its others -0.15 to 0.15, first two translation entries -0.3 to 0.3, third translation entry 4.5 to 6, focal lengths 2 to 3 times 16 max(32, 256 div 32), principal point within 20 of the image centre. `send_blocks`: the 16 numbers for one view, owner and receiving device are distinct. `tile_blocks`: A tile's live entries are distinct and come first, -1 fills the rest, and every tile has at least one live entry. `tile_order`: each tile's row is a permutation of 0 to 511.
All inputs are finite; a program needn't handle non-finite values.
Results may differ from a plain program's by a relative error of at most 0.0003.
Values sent between devices are 32-bit elements; how exact they have to be, the bound alone decides.
A program may use at most 128 MiB of HBM per device.

v0:
```python
import math
import jax
import jax.numpy as jnp
from jax import lax
from jax.sharding import PartitionSpec as P

BLOCK_GAUSSIANS = 32
TX = 32
HIGHEST_PRECISE = lax.Precision.HIGHEST
SH_ZERO = 0.28209479177387814
SH_ONE = 0.4886025119029199
SH_TWO = [
    1.0925484305920792,
    -1.0925484305920792,
    0.31539156525252005,
    -1.0925484305920792,
    0.5462742152960396,
]
SH_THREE = [
    -0.5900435899266435,
    2.890611442640554,
    -0.4570457994644658,
    0.3731763325901154,
    -0.4570457994644658,
    1.445305721320277,
    -0.5900435899266435,
]


def quat_matrix(qw, qx, qy, qz):
    return [
        [1.0 - 2.0 * (qy * qy + qz * qz), 2.0 * (qx * qy - qw * qz), 2.0 * (qx * qz + qw * qy)],
        [2.0 * (qx * qy + qw * qz), 1.0 - 2.0 * (qx * qx + qz * qz), 2.0 * (qy * qz - qw * qx)],
        [2.0 * (qx * qz - qw * qy), 2.0 * (qy * qz + qw * qx), 1.0 - 2.0 * (qx * qx + qy * qy)],
    ]


def sh_basis(dirx, diry, dirz):
    xx, yy, zz = (dirx * dirx, diry * diry, dirz * dirz)
    return [
        SH_ZERO + 0.0 * dirx,
        -SH_ONE * diry,
        SH_ONE * dirz,
        -SH_ONE * dirx,
        SH_TWO[0] * dirx * diry,
        SH_TWO[1] * diry * dirz,
        SH_TWO[2] * (2.0 * zz - xx - yy),
        SH_TWO[3] * dirx * dirz,
        SH_TWO[4] * (xx - yy),
        SH_THREE[0] * diry * (3.0 * xx - yy),
        SH_THREE[1] * dirx * diry * dirz,
        SH_THREE[2] * diry * (4.0 * zz - xx - yy),
        SH_THREE[3] * dirz * (2.0 * zz - 3.0 * xx - 3.0 * yy),
        SH_THREE[4] * dirx * (4.0 * zz - xx - yy),
        SH_THREE[5] * dirz * (xx - yy),
        SH_THREE[6] * dirx * (xx - 3.0 * yy),
    ]


def project(gauss, camera_row):
    cam_norm = jnp.sqrt(jnp.sum(camera_row[0:4] * camera_row[0:4]))
    cam_quat = camera_row[0:4] / cam_norm
    rotation = quat_matrix(cam_quat[0], cam_quat[1], cam_quat[2], cam_quat[3])
    focal_x, focal_y, centre_x, centre_y = (
        camera_row[7],
        camera_row[8],
        camera_row[9],
        camera_row[10],
    )
    cam_pos = [
        rotation[i][0] * gauss[0]
        + rotation[i][1] * gauss[1]
        + rotation[i][2] * gauss[2]
        + camera_row[4 + i]
        for i in range(3)
    ]
    inverse = 1.0 / cam_pos[2]
    screen_u = focal_x * cam_pos[0] * inverse + centre_x
    screen_w = focal_y * cam_pos[1] * inverse + centre_y
    gauss_norm = jnp.sqrt(
        gauss[6] * gauss[6] + gauss[7] * gauss[7] + gauss[8] * gauss[8] + gauss[9] * gauss[9]
    )
    grot = quat_matrix(
        gauss[6] / gauss_norm, gauss[7] / gauss_norm, gauss[8] / gauss_norm, gauss[9] / gauss_norm
    )
    scales = [jnp.exp(gauss[3 + k]) for k in range(3)]
    axes_cam = [
        [
            rotation[i][0] * grot[0][k] + rotation[i][1] * grot[1][k] + rotation[i][2] * grot[2][k]
            for k in range(3)
        ]
        for i in range(3)
    ]
    row_one = [
        (
            focal_x * inverse * axes_cam[0][k]
            - focal_x * cam_pos[0] * inverse * inverse * axes_cam[2][k]
        )
        * scales[k]
        for k in range(3)
    ]
    row_two = [
        (
            focal_y * inverse * axes_cam[1][k]
            - focal_y * cam_pos[1] * inverse * inverse * axes_cam[2][k]
        )
        * scales[k]
        for k in range(3)
    ]
    entry_a = row_one[0] * row_one[0] + row_one[1] * row_one[1] + row_one[2] * row_one[2] + 0.3
    entry_b = row_one[0] * row_two[0] + row_one[1] * row_two[1] + row_one[2] * row_two[2]
    entry_c = row_two[0] * row_two[0] + row_two[1] * row_two[1] + row_two[2] * row_two[2] + 0.3
    determinant = entry_a * entry_c - entry_b * entry_b
    opacity = jax.nn.sigmoid(gauss[10])
    distance = jnp.sqrt(cam_pos[0] * cam_pos[0] + cam_pos[1] * cam_pos[1] + cam_pos[2] * cam_pos[2])
    direction = [
        (rotation[0][j] * cam_pos[0] + rotation[1][j] * cam_pos[1] + rotation[2][j] * cam_pos[2])
        / distance
        for j in range(3)
    ]
    basis = sh_basis(direction[0], direction[1], direction[2])
    colors = []
    for channel in range(3):
        accum = 0.5 + basis[0] * gauss[11 + channel]
        for order in range(1, 16):
            accum = accum + basis[order] * gauss[11 + 3 * order + channel]
        colors.append(jnp.maximum(accum, 0.0))
    return jnp.stack(
        [
            screen_u,
            screen_w,
            entry_c / determinant,
            -entry_b / determinant,
            entry_a / determinant,
            opacity,
        ]
        + colors
    )


def expand(blocks, order):
    tiles_n, width = blocks.shape
    visible = blocks >= 0
    slots = jnp.maximum(blocks, 0)
    inner_product = jnp.arange(BLOCK_GAUSSIANS, dtype=jnp.int32)
    positions = (slots[:, :, None] * BLOCK_GAUSSIANS + inner_product).reshape(
        tiles_n, width * BLOCK_GAUSSIANS
    )
    visible = jnp.broadcast_to(visible[:, :, None], (tiles_n, width, BLOCK_GAUSSIANS)).reshape(
        tiles_n, width * BLOCK_GAUSSIANS
    )
    positions = jnp.take_along_axis(positions, order, axis=1)
    visible = jnp.take_along_axis(visible, order, axis=1)
    return (positions, visible)


def composite(fields, positions, visible, goal, first_tile):
    count, length = positions.shape
    pixels = goal.shape[-1]
    group = math.gcd(count, 4)
    steps_n = count // group
    pixel_ids = jnp.arange(pixels, dtype=jnp.int32)
    offset_x = (pixel_ids % 16).astype(jnp.float32) + 0.5
    offset_y = (pixel_ids // 16).astype(jnp.float32) + 0.5

    def step(carry, item):
        indices, alive, wanted, number = item
        tiles = first_tile + number * group + jnp.arange(group, dtype=jnp.int32)
        pix_x = (tiles % TX * 16).astype(jnp.float32)[:, None] + offset_x
        pix_y = (tiles // TX * 16).astype(jnp.float32)[:, None] + offset_y
        weights_mask = alive.astype(jnp.float32)

        def render(local_part):
            delta_x = pix_x[:, None, :] - local_part[0][:, :, None]
            delta_y = pix_y[:, None, :] - local_part[1][:, :, None]
            power = (
                -0.5
                * (
                    local_part[2][:, :, None] * delta_x * delta_x
                    + local_part[4][:, :, None] * delta_y * delta_y
                )
                - local_part[3][:, :, None] * delta_x * delta_y
            )
            alpha_value = (local_part[5] * weights_mask)[:, :, None] * jnp.exp(power)
            logs = jnp.log1p(-alpha_value)
            transmit_factor = jnp.exp(jnp.cumsum(logs, axis=1) - logs)
            return jnp.einsum(
                "dal,jda->djl",
                alpha_value * transmit_factor,
                local_part[6:9],
                precision=HIGHEST_PRECISE,
            )

        local_part = fields[:, indices]
        color, pullback = jax.vjp(render, local_part)
        local_grad = pullback((color - wanted) / pixels)[0]
        carry = carry.at[:, indices.reshape(-1)].add(local_grad.reshape(local_grad.shape[0], -1))
        return (carry, color)

    items = (
        positions.reshape(steps_n, group, length),
        visible.reshape(steps_n, group, length),
        goal.reshape(steps_n, group, 3, pixels),
        jnp.arange(steps_n, dtype=jnp.int32),
    )
    total, colors = lax.scan(step, jnp.zeros_like(fields), items)
    return (colors.reshape(count, 3, pixels), total)


def local(params, camera, targets, send_blocks, tile_blocks, tile_order):
    cells = lax.axis_size("cell")
    cell_index = lax.axis_index("cell")
    camera_row = camera[0]
    values_n = params.shape[0]
    owned_blocks = params.shape[1] // BLOCK_GAUSSIANS
    per_peer = send_blocks.shape[3]
    width = per_peer * BLOCK_GAUSSIANS
    picks = send_blocks[0, 0].reshape(-1)
    chosen = jnp.take(
        params.reshape(values_n, owned_blocks, BLOCK_GAUSSIANS), picks, axis=1
    ).reshape(values_n, cells * width)
    positions, visible = expand(tile_blocks[0], tile_order[0])
    first_tile = cell_index * tile_blocks.shape[1]
    received = lax.all_to_all(
        chosen.reshape(values_n, cells, width), "cell", split_axis=1, concat_axis=1, tiled=True
    ).reshape(values_n, cells * width)
    arrived, pullback = jax.vjp(lambda gathered: project(gathered, camera_row), received)
    picture, field_grad = composite(arrived, positions, visible, targets[0], first_tile)
    slot_grad = pullback(field_grad)[0]
    sent_grad = lax.all_to_all(
        slot_grad.reshape(values_n, cells, width), "cell", split_axis=1, concat_axis=1, tiled=True
    ).reshape(values_n, cells * width)
    per_block = jnp.transpose(
        sent_grad.reshape(values_n, cells * per_peer, BLOCK_GAUSSIANS), (1, 0, 2)
    )
    summed = jax.ops.segment_sum(per_block, picks, num_segments=owned_blocks)
    summed = jnp.transpose(summed, (1, 0, 2)).reshape(values_n, owned_blocks * BLOCK_GAUSSIANS)
    total = lax.psum(summed, "view")
    return (picture[None], total)


def solution(mesh):
    return jax.shard_map(
        local,
        mesh=mesh,
        in_specs=(
            P(None, "cell"),
            P("view", None),
            P("view", "cell", None, None),
            P("view", "cell", None, None),
            P("view", "cell", None),
            P("view", "cell", None),
        ),
        out_specs=(P("view", "cell", None, None), P(None, "cell")),
        check_vma=False,
    )
```

profile of v0, /device:TPU:0, one launch (start us, length us, event | category | flops | bytes accessed | tf_op | source)
XLA Modules:
  0.0 1059.9 jit_solution(7028042116414189610)
XLA Ops:
  39.2 137.9 %gather_fusion.3 = pred[16384]{0:T(1024)(128)(4,1)S(1)} fusion(pred[32,512]{1,0:T(8,128)(4,1)S(1)} %reshape.6814, s32[16384]{0:T(1024)S(1)} %bitcast.267), kind=kCustom, calls=%fused_computation.3 | custom fusion | bytes 163840 | tf_op jit(solution)/shard_map/jit(take_along_axis)/gather | solution.py:153
  177.6 129.5 %gather_fusion.2 = s32[16384]{0:T(1024)S(1)} fusion(s32[32,512]{1,0:T(8,128)S(1)} %broadcast_add_fusion.4, s32[16384]{0:T(1024)S(1)} %bitcast.268), kind=kCustom, calls=%fused_computation.2 | custom fusion | bytes 262144 | tf_op jit(solution)/shard_map/jit(take_along_axis)/gather | solution.py:152
  331.4 563.3 %while.15 = (s32[]{:T(128)}, f32[9,4096]{0,1:T(8,128)}, f32[8,4,3,256]{3,2,1,0:T(4,128)}, s32[8,4,512]{2,1,0:T(4,128)}, f32[9,4096]{0,1:T(8,128)}, /*index=5*/pr...) while((s32[]{:T(128)}, f32[9,4096]{0,1:T(8,128)}, ...), condition=%wide.region_13.14_spmd.clone, body=%wide.region_1.13_spmd.clone.sunk | while | flops 240312416 | bytes 65026284 | solution.py:206
  377.0 9.6 fusion.187
  391.6 7.6 fusion.188
  400.8 12.2 %scatter_fusion = f32[9,4096]{0,1:T(8,128)S(1)} fusion(f32[9,4096]{0,1:T(8,128)S(1)} %copy-done.2, s32[2048]{0:T(1024)S(1)} %bitcast.313, f32[2048,9]{1,0:T(8,128)S(1)} %copy.228), kind=kCustom, calls=%fused_computation.4.clone.clone.1 | custom fusion | flops 18432 | bytes 229376 | tf_op jit(solution)/shard_map/while/body/eval_jaxpr/scatter-add | solution.py:197
  445.6 9.6 fusion.187
  460.2 7.6 fusion.188
  469.4 12.2 %scatter_fusion = f32[9,4096]{0,1:T(8,128)S(1)} fusion(f32[9,4096]{0,1:T(8,128)S(1)} %copy-done.2, s32[2048]{0:T(1024)S(1)} %bitcast.313, f32[2048,9]{1,0:T(8,128)S(1)} %copy.228), kind=kCustom, calls=%fused_computation.4.clone.clone.1 | custom fusion | flops 18432 | bytes 229376 | tf_op jit(solution)/shard_map/while/body/eval_jaxpr/scatter-add | solution.py:197
  514.3 9.6 fusion.187
  538.0 12.2 %scatter_fusion = f32[9,4096]{0,1:T(8,128)S(1)} fusion(f32[9,4096]{0,1:T(8,128)S(1)} %copy-done.2, s32[2048]{0:T(1024)S(1)} %bitcast.313, f32[2048,9]{1,0:T(8,128)S(1)} %copy.228), kind=kCustom, calls=%fused_computation.4.clone.clone.1 | custom fusion | flops 18432 | bytes 229376 | tf_op jit(solution)/shard_map/while/body/eval_jaxpr/scatter-add | solution.py:197
  582.8 9.6 fusion.187
  606.6 12.2 %scatter_fusion = f32[9,4096]{0,1:T(8,128)S(1)} fusion(f32[9,4096]{0,1:T(8,128)S(1)} %copy-done.2, s32[2048]{0:T(1024)S(1)} %bitcast.313, f32[2048,9]{1,0:T(8,128)S(1)} %copy.228), kind=kCustom, calls=%fused_computation.4.clone.clone.1 | custom fusion | flops 18432 | bytes 229376 | tf_op jit(solution)/shard_map/while/body/eval_jaxpr/scatter-add | solution.py:197
  651.4 9.6 fusion.187
  675.2 12.2 %scatter_fusion = f32[9,4096]{0,1:T(8,128)S(1)} fusion(f32[9,4096]{0,1:T(8,128)S(1)} %copy-done.2, s32[2048]{0:T(1024)S(1)} %bitcast.313, f32[2048,9]{1,0:T(8,128)S(1)} %copy.228), kind=kCustom, calls=%fused_computation.4.clone.clone.1 | custom fusion | flops 18432 | bytes 229376 | tf_op jit(solution)/shard_map/while/body/eval_jaxpr/scatter-add | solution.py:197
  720.1 9.6 fusion.187
  743.9 12.2 %scatter_fusion = f32[9,4096]{0,1:T(8,128)S(1)} fusion(f32[9,4096]{0,1:T(8,128)S(1)} %copy-done.2, s32[2048]{0:T(1024)S(1)} %bitcast.313, f32[2048,9]{1,0:T(8,128)S(1)} %copy.228), kind=kCustom, calls=%fused_computation.4.clone.clone.1 | custom fusion | flops 18432 | bytes 229376 | tf_op jit(solution)/shard_map/while/body/eval_jaxpr/scatter-add | solution.py:197
  788.7 9.6 fusion.187
  812.5 12.2 %scatter_fusion = f32[9,4096]{0,1:T(8,128)S(1)} fusion(f32[9,4096]{0,1:T(8,128)S(1)} %copy-done.2, s32[2048]{0:T(1024)S(1)} %bitcast.313, f32[2048,9]{1,0:T(8,128)S(1)} %copy.228), kind=kCustom, calls=%fused_computation.4.clone.clone.1 | custom fusion | flops 18432 | bytes 229376 | tf_op jit(solution)/shard_map/while/body/eval_jaxpr/scatter-add | solution.py:197
  857.3 9.6 fusion.187
  881.1 12.2 %scatter_fusion = f32[9,4096]{0,1:T(8,128)S(1)} fusion(f32[9,4096]{0,1:T(8,128)S(1)} %copy-done.2, s32[2048]{0:T(1024)S(1)} %bitcast.313, f32[2048,9]{1,0:T(8,128)S(1)} %copy.228), kind=kCustom, calls=%fused_computation.4.clone.clone.1 | custom fusion | flops 18432 | bytes 229376 | tf_op jit(solution)/shard_map/while/body/eval_jaxpr/scatter-add | solution.py:197
  926.1 15.2 %all-to-all-done.1 = f32[59,8,512]{2,0,1:T(8,128)S(1)} async-done(((f32[59,8,512]{2,0,1:T(8,128)}), f32[59,8,512]{2,0,1:T(8,128)S(1)}, u32[]{:S(2)}, u32[]{:S(2)}) %all-to-all-start.1) | async-done | bytes 966688 | tf_op jit(solution)/shard_map/all_to_all | solution.py:230
  944.5 15.5 %scatter_fusion.1 = f32[256,59,32]{1,2,0:T(8,128)} fusion(f32[256,59,32]{1,2,0:T(8,128)} %broadcast_in_dim.76, s32[128]{0:T(128)S(1)} %reshape.6864, f32[128,59,32]{1,2,0:T(8,128)S(1)} %bitcast.272), kind=kCustom, calls=%fused_computation.5 | custom fusion | flops 241664 | bytes 2900480 | tf_op jit(solution)/shard_map/scatter-add | solution.py:236
  965.4 84.2 %all-reduce.78.cloned.1.call-done = f32[59,8192]{1,0:T(8,128)} async-done(((f32[59,8192]{1,0:T(8,128)}), f32[59,8192]{1,0:T(8,128)}) %all-reduce.78.cloned.1.call-update) | async-done | bytes 1933328 | tf_op jit(solution)/shard_map/psum | solution.py:238
  (1001 shorter events, 436.8 us)
Async XLA Ops:
  20.5 289.3 %all-to-all-start = ((f32[59,8,512]{2,0,1:T(8,128)}), f32[59,8,512]{2,0,1:T(8,128)S(1)}, u32[]{:S(2)}, u32[]{:S(2)}) async-start(f32[59,8,512]{2,0,1:T(8,128)} %copy.134), calls=%async_computation | async-start | bytes 2097152 | tf_op jit(solution)/shard_map/all_to_all | solution.py:224
  177.6 129.5 %copy-start.117 = (f32[1,32,3,256]{3,1,2,0:T(8,128)S(1)}, f32[1,32,3,256]{3,1,2,0:T(8,128)}, u32[]{:S(2)}) copy-start(f32[1,32,3,256]{3,1,2,0:T(8,128)} %param.10) | copy-start | bytes 294916
  310.7 15.4 %copy-start.28 = (f32[1,8,512]{2,0,1:T(1,128)}, f32[1,8,512]{2,0,1:T(1,128)S(1)}, u32[]{:S(2)}) copy-start(f32[1,8,512]{2,0,1:T(1,128)S(1)} %get-tuple-element.415) | copy-start | bytes 49156
  894.8 13.4 %copy-start.33 = (f32[1,4096]{1,0:T(1,128)S(1)}, f32[1,4096]{1,0:T(1,128)}, u32[]{:S(2)}) copy-start(f32[1,4096]{1,0:T(1,128)} %copy-done.32) | copy-start | bytes 49156
  894.8 13.4 %copy-start.35 = (f32[1,4096]{1,0:T(1,128)S(1)}, f32[1,4096]{1,0:T(1,128)}, u32[]{:S(2)}) copy-start(f32[1,4096]{1,0:T(1,128)} %copy-done.34) | copy-start | bytes 49156
  894.8 13.4 %copy-start.37 = (f32[1,4096]{1,0:T(1,128)S(1)}, f32[1,4096]{1,0:T(1,128)}, u32[]{:S(2)}) copy-start(f32[1,4096]{1,0:T(1,128)} %copy-done.36) | copy-start | bytes 49156
  894.8 13.4 %copy-start.39 = (f32[1,4096]{1,0:T(1,128)S(1)}, f32[1,4096]{1,0:T(1,128)}, u32[]{:S(2)}) copy-start(f32[1,4096]{1,0:T(1,128)} %copy-done.38) | copy-start | bytes 49156
  894.8 13.4 %copy-start.45 = (f32[1,4096]{1,0:T(1,128)S(1)}, f32[1,4096]{1,0:T(1,128)}, u32[]{:S(2)}) copy-start(f32[1,4096]{1,0:T(1,128)} %copy-done.44) | copy-start | bytes 49156
  894.8 13.4 %copy-start.47 = (f32[1,4096]{1,0:T(1,128)S(1)}, f32[1,4096]{1,0:T(1,128)}, u32[]{:S(2)}) copy-start(f32[1,4096]{1,0:T(1,128)} %copy-done.46) | copy-start | bytes 49156
  894.9 13.4 %copy-start.49 = (f32[1,4096]{1,0:T(1,128)S(1)}, f32[1,4096]{1,0:T(1,128)}, u32[]{:S(2)}) copy-start(f32[1,4096]{1,0:T(1,128)} %copy-done.48) | copy-start | bytes 49156
  897.1 12.8 %copy-start.43 = (f32[1,4096]{1,0:T(1,128)S(1)}, f32[1,4096]{1,0:T(1,128)}, u32[]{:S(2)}) copy-start(f32[1,4096]{1,0:T(1,128)} %get-tuple-element.333) | copy-start | bytes 49156
  897.2 12.8 %copy-start.51 = (f32[1,8,512]{2,0,1:T(1,128)S(1)}, f32[1,8,512]{2,0,1:T(1,128)}, u32[]{:S(2)}) copy-start(f32[1,8,512]{2,0,1:T(1,128)} %copy-done.50) | copy-start | bytes 49156
  897.2 12.8 %copy-start.70 = (f32[1,8,512]{2,0,1:T(1,128)S(1)}, f32[1,8,512]{2,0,1:T(1,128)}, u32[]{:S(2)}) copy-start(f32[1,8,512]{2,0,1:T(1,128)} %copy-done.69) | copy-start | bytes 49156
  897.2 12.8 %copy-start.72 = (f32[1,8,512]{2,0,1:T(1,128)S(1)}, f32[1,8,512]{2,0,1:T(1,128)}, u32[]{:S(2)}) copy-start(f32[1,8,512]{2,0,1:T(1,128)} %copy-done.71) | copy-start | bytes 49156
  897.2 12.8 %copy-start.74 = (f32[1,8,512]{2,0,1:T(1,128)S(1)}, f32[1,8,512]{2,0,1:T(1,128)}, u32[]{:S(2)}) copy-start(f32[1,8,512]{2,0,1:T(1,128)} %copy-done.73) | copy-start | bytes 49156
  897.2 12.8 %copy-start.76 = (f32[1,8,512]{2,0,1:T(1,128)S(1)}, f32[1,8,512]{2,0,1:T(1,128)}, u32[]{:S(2)}) copy-start(f32[1,8,512]{2,0,1:T(1,128)} %copy-done.75) | copy-start | bytes 49156
  897.2 12.8 %copy-start.78 = (f32[1,8,512]{2,0,1:T(1,128)S(1)}, f32[1,8,512]{2,0,1:T(1,128)}, u32[]{:S(2)}) copy-start(f32[1,8,512]{2,0,1:T(1,128)} %copy-done.77) | copy-start | bytes 49156
  897.2 12.8 %copy-start.80 = (f32[1,8,512]{2,0,1:T(1,128)S(1)}, f32[1,8,512]{2,0,1:T(1,128)}, u32[]{:S(2)}) copy-start(f32[1,8,512]{2,0,1:T(1,128)} %copy-done.79) | copy-start | bytes 49156
  897.2 12.8 %copy-start.82 = (f32[1,8,512]{2,0,1:T(1,128)S(1)}, f32[1,8,512]{2,0,1:T(1,128)}, u32[]{:S(2)}) copy-start(f32[1,8,512]{2,0,1:T(1,128)} %copy-done.81) | copy-start | bytes 49156
  897.2 12.8 %copy-start.84 = (f32[1,8,512]{2,0,1:T(1,128)S(1)}, f32[1,8,512]{2,0,1:T(1,128)}, u32[]{:S(2)}) copy-start(f32[1,8,512]{2,0,1:T(1,128)} %copy-done.83) | copy-start | bytes 49156
  897.2 12.8 %copy-start.86 = (f32[1,8,512]{2,0,1:T(1,128)S(1)}, f32[1,8,512]{2,0,1:T(1,128)}, u32[]{:S(2)}) copy-start(f32[1,8,512]{2,0,1:T(1,128)} %copy-done.85) | copy-start | bytes 49156
  897.3 12.8 %copy-start.88 = (f32[1,8,512]{2,0,1:T(1,128)S(1)}, f32[1,8,512]{2,0,1:T(1,128)}, u32[]{:S(2)}) copy-start(f32[1,8,512]{2,0,1:T(1,128)} %copy-done.87) | copy-start | bytes 49156
  921.7 19.6 %all-to-all-start.1 = ((f32[59,8,512]{2,0,1:T(8,128)}), f32[59,8,512]{2,0,1:T(8,128)S(1)}, u32[]{:S(2)}, u32[]{:S(2)}) async-start(f32[59,8,512]{2,0,1:T(8,128)} %copy.150), calls=%async_computation.1 | async-start | bytes 2097152 | tf_op jit(solution)/shard_map/all_to_all | solution.py:230
  925.9 123.6 %all-reduce.78.cloned.1.call-start = ((), (), s32[]{:S(2)}) async-start(), calls=%async_computation.2 | async-start | bytes 4194304 | tf_op jit(solution)/shard_map/psum | solution.py:238
  (226 other events, 813.5 us)
Sparse Core Ops, SparseCore 0:
  964.0 85.5 all-reduce.77
where the time goes:
time: 1070 us; the launch traced here: 1060 us
  local copies, waits for them, and re-layouts  444 us (41%)
  other arithmetic  374 us (35%)
  waiting for transfers between devices  99.4 us (9%)
  matrix products  82.1 us (8%)
  between operations  27.9 us (3%)
  loops' own time  23 us (2%)
    gather x2, local copies, waits for them, and re-layouts, expand(): visible = jnp.take_along_axis(visible, order, axis=1)  138 us
    another operation x48, other arithmetic  134 us
    gather x2, local copies, waits for them, and re-layouts, expand(): positions = jnp.take_along_axis(positions, order, axis=1)  129 us
    scatter-add x8, other arithmetic, step(): carry.at[:, indices.reshape(-1)]  97.8 us
    psum x1, waiting for transfers between devices, local(): total = lax.psum(summed, 'view')  84.2 us
    dot_general x24, matrix products, render(): jnp.einsum('dal,jda->djl', alpha_value * transmit_factor, local_part[6:9]...  82.1 us
    reduce_sum x8, other arithmetic, render(): local_part[3][:, :, None] * delta_x * delta_y  60.7 us
    gather x16, local copies, waits for them, and re-layouts, step(): local_part = fields[:, indices]  59 us
  transfers between devices with their start and end apart: 3, of which 2 were waited for; matrix products, arithmetic and copies ran while one was open for 26% of the time, Pallas kernels for 0%

commit v1 on v0

--- a/solution.py
+++ b/solution.py
@@ -235,7 +235,9 @@
     )
     summed = jax.ops.segment_sum(per_block, picks, num_segments=owned_blocks)
     summed = jnp.transpose(summed, (1, 0, 2)).reshape(values_n, owned_blocks * BLOCK_GAUSSIANS)
-    total = lax.psum(summed, "view")
+    total = summed
+    for hop in (1, 2):
+        total = total + lax.ppermute(total, "view", [(dev, dev ^ hop) for dev in range(4)])
     return (picture[None], total)
 
 

time: 1070 us -> 1110 us (1.037)
  waiting for transfers between devices: 99.4 us -> 144 us
  between operations: 27.9 us -> 15 us
    ppermute x0 -> x2, waiting for transfers between devices: none -> 129 us  [local(): lax.ppermute(total, 'view', [(dev, dev ^ hop) for dev in range(4)])]
    psum x1 -> x0, waiting for transfers between devices: 84.2 us -> none  [local(): total = lax.psum(summed, 'view')]
  transfers between devices with their start and end apart: 3 -> 4, of which waited for: 2 -> 3; matrix products, arithmetic and copies ran while one was open for 26% -> 25% of each run, Pallas kernels for 0% -> 0%
where the time goes in v1:
time: 1110 us; the launch traced here: 1090 us
  local copies, waits for them, and re-layouts  440 us (40%)
  other arithmetic  375 us (34%)
  waiting for transfers between devices  144 us (13%)
  matrix products  81.8 us (7%)
  loops' own time  23.3 us (2%)
  between operations  15 us (1%)
  starting transfers between devices  14.6 us (1%)
    gather x2, local copies, waits for them, and re-layouts, expand(): visible = jnp.take_along_axis(visible, order, axis=1)  138 us
    another operation x48, other arithmetic  134 us
    gather x2, local copies, waits for them, and re-layouts, expand(): positions = jnp.take_along_axis(positions, order, axis=1)  129 us
    ppermute x2, waiting for transfers between devices, local(): lax.ppermute(total, 'view', [(dev, dev ^ hop) for dev in range(4)])  129 us
    scatter-add x8, other arithmetic, step(): carry.at[:, indices.reshape(-1)]  97.8 us
    dot_general x24, matrix products, render(): jnp.einsum('dal,jda->djl', alpha_value * transmit_factor, local_part[6:9]...  81.8 us
    reduce_sum x8, other arithmetic, render(): local_part[3][:, :, None] * delta_x * delta_y  60.7 us
    gather x16, local copies, waits for them, and re-layouts, step(): local_part = fields[:, indices]  59 us
  transfers between devices with their start and end apart: 4, of which 3 were waited for; matrix products, arithmetic and copies ran while one was open for 25% of the time, Pallas kernels for 0%

profile of v1, /device:TPU:0, one launch (start us, length us, event | category | flops | bytes accessed | tf_op | source)
XLA Modules:
  0.0 1093.7 jit_solution(8785311185021395666)
XLA Ops:
  33.2 137.9 %gather_fusion.3 = pred[16384]{0:T(1024)(128)(4,1)S(1)} fusion(pred[32,512]{1,0:T(8,128)(4,1)S(1)} %reshape.6814, s32[16384]{0:T(1024)S(1)} %bitcast.267), kind=kCustom, calls=%fused_computation.3 | custom fusion | bytes 163840 | tf_op jit(solution)/shard_map/jit(take_along_axis)/gather | solution.py:153
  171.6 129.5 %gather_fusion.2 = s32[16384]{0:T(1024)S(1)} fusion(s32[32,512]{1,0:T(8,128)S(1)} %broadcast_add_fusion.4, s32[16384]{0:T(1024)S(1)} %bitcast.268), kind=kCustom, calls=%fused_computation.2 | custom fusion | bytes 262144 | tf_op jit(solution)/shard_map/jit(take_along_axis)/gather | solution.py:152
  325.3 563.9 %while.15 = (s32[]{:T(128)}, f32[9,4096]{0,1:T(8,128)}, f32[8,4,3,256]{3,2,1,0:T(4,128)}, s32[8,4,512]{2,1,0:T(4,128)}, f32[9,4096]{0,1:T(8,128)}, /*index=5*/pr...) while((s32[]{:T(128)}, f32[9,4096]{0,1:T(8,128)}, ...), condition=%wide.region_13.14_spmd.clone, body=%wide.region_1.13_spmd.clone.sunk | while | flops 240312416 | bytes 65026284 | solution.py:206
  371.1 9.6 fusion.187
  385.6 7.6 fusion.188
  394.8 12.2 %scatter_fusion = f32[9,4096]{0,1:T(8,128)S(1)} fusion(f32[9,4096]{0,1:T(8,128)S(1)} %copy-done.2, s32[2048]{0:T(1024)S(1)} %bitcast.313, f32[2048,9]{1,0:T(8,128)S(1)} %copy.233), kind=kCustom, calls=%fused_computation.4.clone.clone.1 | custom fusion | flops 18432 | bytes 229376 | tf_op jit(solution)/shard_map/while/body/eval_jaxpr/scatter-add | solution.py:197
  439.7 9.6 fusion.187
  463.5 12.2 %scatter_fusion = f32[9,4096]{0,1:T(8,128)S(1)} fusion(f32[9,4096]{0,1:T(8,128)S(1)} %copy-done.2, s32[2048]{0:T(1024)S(1)} %bitcast.313, f32[2048,9]{1,0:T(8,128)S(1)} %copy.233), kind=kCustom, calls=%fused_computation.4.clone.clone.1 | custom fusion | flops 18432 | bytes 229376 | tf_op jit(solution)/shard_map/while/body/eval_jaxpr/scatter-add | solution.py:197
  508.4 9.6 fusion.187
  532.2 12.2 %scatter_fusion = f32[9,4096]{0,1:T(8,128)S(1)} fusion(f32[9,4096]{0,1:T(8,128)S(1)} %copy-done.2, s32[2048]{0:T(1024)S(1)} %bitcast.313, f32[2048,9]{1,0:T(8,128)S(1)} %copy.233), kind=kCustom, calls=%fused_computation.4.clone.clone.1 | custom fusion | flops 18432 | bytes 229376 | tf_op jit(solution)/shard_map/while/body/eval_jaxpr/scatter-add | solution.py:197
  577.1 9.6 fusion.187
  600.9 12.2 %scatter_fusion = f32[9,4096]{0,1:T(8,128)S(1)} fusion(f32[9,4096]{0,1:T(8,128)S(1)} %copy-done.2, s32[2048]{0:T(1024)S(1)} %bitcast.313, f32[2048,9]{1,0:T(8,128)S(1)} %copy.233), kind=kCustom, calls=%fused_computation.4.clone.clone.1 | custom fusion | flops 18432 | bytes 229376 | tf_op jit(solution)/shard_map/while/body/eval_jaxpr/scatter-add | solution.py:197
  645.8 9.6 fusion.187
  669.6 12.2 %scatter_fusion = f32[9,4096]{0,1:T(8,128)S(1)} fusion(f32[9,4096]{0,1:T(8,128)S(1)} %copy-done.2, s32[2048]{0:T(1024)S(1)} %bitcast.313, f32[2048,9]{1,0:T(8,128)S(1)} %copy.233), kind=kCustom, calls=%fused_computation.4.clone.clone.1 | custom fusion | flops 18432 | bytes 229376 | tf_op jit(solution)/shard_map/while/body/eval_jaxpr/scatter-add | solution.py:197
  714.5 9.6 fusion.187
  738.3 12.2 %scatter_fusion = f32[9,4096]{0,1:T(8,128)S(1)} fusion(f32[9,4096]{0,1:T(8,128)S(1)} %copy-done.2, s32[2048]{0:T(1024)S(1)} %bitcast.313, f32[2048,9]{1,0:T(8,128)S(1)} %copy.233), kind=kCustom, calls=%fused_computation.4.clone.clone.1 | custom fusion | flops 18432 | bytes 229376 | tf_op jit(solution)/shard_map/while/body/eval_jaxpr/scatter-add | solution.py:197
  783.2 9.6 fusion.187
  807.0 12.2 %scatter_fusion = f32[9,4096]{0,1:T(8,128)S(1)} fusion(f32[9,4096]{0,1:T(8,128)S(1)} %copy-done.2, s32[2048]{0:T(1024)S(1)} %bitcast.313, f32[2048,9]{1,0:T(8,128)S(1)} %copy.233), kind=kCustom, calls=%fused_computation.4.clone.clone.1 | custom fusion | flops 18432 | bytes 229376 | tf_op jit(solution)/shard_map/while/body/eval_jaxpr/scatter-add | solution.py:197
  851.9 9.6 fusion.187
  875.7 12.2 %scatter_fusion = f32[9,4096]{0,1:T(8,128)S(1)} fusion(f32[9,4096]{0,1:T(8,128)S(1)} %copy-done.2, s32[2048]{0:T(1024)S(1)} %bitcast.313, f32[2048,9]{1,0:T(8,128)S(1)} %copy.233), kind=kCustom, calls=%fused_computation.4.clone.clone.1 | custom fusion | flops 18432 | bytes 229376 | tf_op jit(solution)/shard_map/while/body/eval_jaxpr/scatter-add | solution.py:197
  920.1 15.3 %all-to-all-done.1 = f32[59,8,512]{2,0,1:T(8,128)S(1)} async-done(((f32[59,8,512]{2,0,1:T(8,128)}), f32[59,8,512]{2,0,1:T(8,128)S(1)}, u32[]{:S(2)}, u32[]{:S(2)}) %all-to-all-start.1) | async-done | bytes 966688 | tf_op jit(solution)/shard_map/all_to_all | solution.py:230
  938.6 15.5 %scatter_fusion.1 = f32[256,59,32]{1,2,0:T(8,128)} fusion(f32[256,59,32]{1,2,0:T(8,128)} %broadcast_in_dim.76, s32[128]{0:T(128)S(1)} %reshape.6864, f32[128,59,32]{1,2,0:T(8,128)S(1)} %bitcast.272), kind=kCustom, calls=%fused_computation.5 | custom fusion | flops 241664 | bytes 2900480 | tf_op jit(solution)/shard_map/scatter-add | solution.py:236
  958.6 43.1 %collective-permute-done = f32[59,8192]{1,0:T(8,128)S(1)} collective-permute-done((f32[59,8192]{1,0:T(8,128)S(1)}, f32[59,8192]{1,0:T(8,128)S(1)}, u32[]{:S(2)}, u32[]{:S(2)}) %collective-permute-start) | collective-permute-done | bytes 1933344 | tf_op jit(solution)/shard_map/ppermute | solution.py:240
  1006.2 85.5 %collective-permute-done.1 = f32[59,8192]{1,0:T(8,128)S(1)} collective-permute-done((f32[59,8192]{1,0:T(8,128)S(1)}, f32[59,8192]{1,0:T(8,128)S(1)}, u32[]{:S(2)}, u32[]{:S(2)}) %collective-permute-start.1) | collective-permute-done | bytes 1933344 | tf_op jit(solution)/shard_map/ppermute | solution.py:240
  (1003 shorter events, 446.2 us)
Async XLA Ops:
  14.0 289.8 %all-to-all-start = ((f32[59,8,512]{2,0,1:T(8,128)}), f32[59,8,512]{2,0,1:T(8,128)S(1)}, u32[]{:S(2)}, u32[]{:S(2)}) async-start(f32[59,8,512]{2,0,1:T(8,128)} %copy.138), calls=%async_computation | async-start | bytes 2097152 | tf_op jit(solution)/shard_map/all_to_all | solution.py:224
  171.6 129.5 %copy-start.117 = (f32[1,32,3,256]{3,1,2,0:T(8,128)S(1)}, f32[1,32,3,256]{3,1,2,0:T(8,128)}, u32[]{:S(2)}) copy-start(f32[1,32,3,256]{3,1,2,0:T(8,128)} %param.10) | copy-start | bytes 294916
  304.8 15.3 %copy-start.28 = (f32[1,8,512]{2,0,1:T(1,128)}, f32[1,8,512]{2,0,1:T(1,128)S(1)}, u32[]{:S(2)}) copy-start(f32[1,8,512]{2,0,1:T(1,128)S(1)} %get-tuple-element.415) | copy-start | bytes 49156
  307.6 12.5 %copy-start.50 = (f32[1,8,512]{2,0,1:T(1,128)}, f32[1,8,512]{2,0,1:T(1,128)S(1)}, u32[]{:S(2)}) copy-start(f32[1,8,512]{2,0,1:T(1,128)S(1)} %get-tuple-element.416) | copy-start | bytes 49156
  889.4 13.1 %copy-start.33 = (f32[1,4096]{1,0:T(1,128)S(1)}, f32[1,4096]{1,0:T(1,128)}, u32[]{:S(2)}) copy-start(f32[1,4096]{1,0:T(1,128)} %copy-done.32) | copy-start | bytes 49156
  889.4 13.1 %copy-start.35 = (f32[1,4096]{1,0:T(1,128)S(1)}, f32[1,4096]{1,0:T(1,128)}, u32[]{:S(2)}) copy-start(f32[1,4096]{1,0:T(1,128)} %copy-done.34) | copy-start | bytes 49156
  889.4 13.1 %copy-start.37 = (f32[1,4096]{1,0:T(1,128)S(1)}, f32[1,4096]{1,0:T(1,128)}, u32[]{:S(2)}) copy-start(f32[1,4096]{1,0:T(1,128)} %copy-done.36) | copy-start | bytes 49156
  889.4 13.1 %copy-start.39 = (f32[1,4096]{1,0:T(1,128)S(1)}, f32[1,4096]{1,0:T(1,128)}, u32[]{:S(2)}) copy-start(f32[1,4096]{1,0:T(1,128)} %copy-done.38) | copy-start | bytes 49156
  889.4 13.1 %copy-start.45 = (f32[1,4096]{1,0:T(1,128)S(1)}, f32[1,4096]{1,0:T(1,128)}, u32[]{:S(2)}) copy-start(f32[1,4096]{1,0:T(1,128)} %copy-done.44) | copy-start | bytes 49156
  889.4 13.1 %copy-start.47 = (f32[1,4096]{1,0:T(1,128)S(1)}, f32[1,4096]{1,0:T(1,128)}, u32[]{:S(2)}) copy-start(f32[1,4096]{1,0:T(1,128)} %copy-done.46) | copy-start | bytes 49156
  889.4 13.1 %copy-start.49 = (f32[1,4096]{1,0:T(1,128)S(1)}, f32[1,4096]{1,0:T(1,128)}, u32[]{:S(2)}) copy-start(f32[1,4096]{1,0:T(1,128)} %copy-done.48) | copy-start | bytes 49156
  891.7 12.5 %copy-start.43 = (f32[1,4096]{1,0:T(1,128)S(1)}, f32[1,4096]{1,0:T(1,128)}, u32[]{:S(2)}) copy-start(f32[1,4096]{1,0:T(1,128)} %get-tuple-element.333) | copy-start | bytes 49156
  891.7 12.5 %copy-start.51 = (f32[1,8,512]{2,0,1:T(1,128)S(1)}, f32[1,8,512]{2,0,1:T(1,128)}, u32[]{:S(2)}) copy-start(f32[1,8,512]{2,0,1:T(1,128)} %copy-done.50) | copy-start | bytes 49156
  891.7 12.5 %copy-start.70 = (f32[1,8,512]{2,0,1:T(1,128)S(1)}, f32[1,8,512]{2,0,1:T(1,128)}, u32[]{:S(2)}) copy-start(f32[1,8,512]{2,0,1:T(1,128)} %copy-done.69) | copy-start | bytes 49156
  891.7 12.5 %copy-start.72 = (f32[1,8,512]{2,0,1:T(1,128)S(1)}, f32[1,8,512]{2,0,1:T(1,128)}, u32[]{:S(2)}) copy-start(f32[1,8,512]{2,0,1:T(1,128)} %copy-done.71) | copy-start | bytes 49156
  891.8 12.5 %copy-start.74 = (f32[1,8,512]{2,0,1:T(1,128)S(1)}, f32[1,8,512]{2,0,1:T(1,128)}, u32[]{:S(2)}) copy-start(f32[1,8,512]{2,0,1:T(1,128)} %copy-done.73) | copy-start | bytes 49156
  891.8 12.5 %copy-start.76 = (f32[1,8,512]{2,0,1:T(1,128)S(1)}, f32[1,8,512]{2,0,1:T(1,128)}, u32[]{:S(2)}) copy-start(f32[1,8,512]{2,0,1:T(1,128)} %copy-done.75) | copy-start | bytes 49156
  891.8 12.5 %copy-start.78 = (f32[1,8,512]{2,0,1:T(1,128)S(1)}, f32[1,8,512]{2,0,1:T(1,128)}, u32[]{:S(2)}) copy-start(f32[1,8,512]{2,0,1:T(1,128)} %copy-done.77) | copy-start | bytes 49156
  891.8 12.5 %copy-start.80 = (f32[1,8,512]{2,0,1:T(1,128)S(1)}, f32[1,8,512]{2,0,1:T(1,128)}, u32[]{:S(2)}) copy-start(f32[1,8,512]{2,0,1:T(1,128)} %copy-done.79) | copy-start | bytes 49156
  891.8 12.5 %copy-start.82 = (f32[1,8,512]{2,0,1:T(1,128)S(1)}, f32[1,8,512]{2,0,1:T(1,128)}, u32[]{:S(2)}) copy-start(f32[1,8,512]{2,0,1:T(1,128)} %copy-done.81) | copy-start | bytes 49156
  915.8 19.6 %all-to-all-start.1 = ((f32[59,8,512]{2,0,1:T(8,128)}), f32[59,8,512]{2,0,1:T(8,128)S(1)}, u32[]{:S(2)}, u32[]{:S(2)}) async-start(f32[59,8,512]{2,0,1:T(8,128)} %copy.154), calls=%async_computation.1 | async-start | bytes 2097152 | tf_op jit(solution)/shard_map/all_to_all | solution.py:230
  957.0 48.6 %copy-start.116 = (f32[8,4,3,256]{3,2,1,0:T(4,128)S(1)}, f32[8,4,3,256]{3,2,1,0:T(4,128)}, u32[]{:S(2)}) copy-start(f32[8,4,3,256]{3,2,1,0:T(4,128)} %get-tuple-element.143) | copy-start | bytes 294916
  957.0 44.7 %collective-permute-start = (f32[59,8192]{1,0:T(8,128)S(1)}, f32[59,8192]{1,0:T(8,128)S(1)}, u32[]{:S(2)}, u32[]{:S(2)}) collective-permute-start(f32[59,8192]{1,0:T(8,128)S(1)} %copy.157), channel_id=1, source_target_pairs={{0,8},{8,0},{16,24},{24,16},{1,9},{9,1},{17,25},{25,17},{2,10},{10... | collective-permute-start | bytes 5799944 | tf_op jit(solution)/shard_map/ppermute | solution.py:240
  1002.0 89.7 %collective-permute-start.1 = (f32[59,8192]{1,0:T(8,128)S(1)}, f32[59,8192]{1,0:T(8,128)S(1)}, u32[]{:S(2)}, u32[]{:S(2)}) collective-permute-start(f32[59,8192]{1,0:T(8,128)S(1)} %add.8886), channel_id=1, source_target_pairs={{0,16},{8,24},{16,0},{24,8},{1,17},{9,25},{17,1},{25,9},{2,18},{10... | collective-permute-start | bytes 5799944 | tf_op jit(solution)/shard_map/ppermute | solution.py:240
  (227 other events, 834.2 us)
